TPU v7x, 128 devices: a whole 4x4x4 slice. The times are simulated.
128 devices in a mesh: seg: 8 (over z, x_hi), lines: 16 (over x_lo, y, core).
Axes of the slice: x: 4 (x_hi: 2, x_lo: 2; x = x_hi * 2 + x_lo), y: 4, z: 4, core: 2. Of those that a mesh axis runs over, the one named last changes fastest.
Arguments:
- left_features: bfloat16 [64, 8192, 128], P('lines', 'seg'), may hold values from -400 to 400
- right_features: bfloat16 [64, 8192, 128], P('lines', 'seg'), may hold values from -6 to 6
- conv_weight: bfloat16 [3, 3, 3, 128, 128], replicated, may hold values from -0.1875 to 0.1875
- conv_bias: float32 [3, 128], replicated, may hold values from -3 to 3
Outputs:
- refined: bfloat16 [64, 8192, 128], P('lines', 'seg')
- disparity: float32 [64, 8192], P('lines', 'seg')
All inputs are finite; a program needn't handle non-finite values.
Results may differ from a plain program's by a relative error of at most 0.006.
Values may be sent and summed in bfloat16 or wider, within the bound.
A program may use at most 128 MiB of HBM per device.

v0:
```python
import functools
import math

import jax
import jax.numpy as jnp
from jax import lax
from jax.experimental import pallas as pl
from jax.experimental.pallas import tpu as pltpu
from jax.sharding import PartitionSpec as P

NEG = -1e30
LOG2E = 1.4426950408889634
PAD = 16
REACH = 3
MESH = pl.DeviceIdType.MESH
F32 = jnp.float32
BF16 = jnp.bfloat16


def nt_dot(a, b):
    return lax.dot_general(a, b, (((1,), (1,)), ((), ())), preferred_element_type=F32)


def groups(x):
    return x.reshape(x.shape[0] // 8, 8, x.shape[1])


def body(
    shape, left_hbm, right_hbm, w_hbm, bias_ref, out_ref, disp_ref,
    left_v, right_v, tcol, s_ref, own_mt, halo_mt, own_in, halo_in, c1, c2acc,
    own_c2, halo_c2, own_c2_in, halo_c2_in, w_v, wbig, x0, x1, x2, y_ref,
    load_sem, wsem, halo_ss, halo_rs, mt_ss, mt_rs, c2_ss, c2_rs, ln_ss, ln_rs,
):
    segs, line_devs, lines, n, blk, chans, layers = shape
    nblk = n // blk
    win = n + blk
    wide = n + 2 * PAD
    scale = LOG2E / math.sqrt(chans)
    seg = lax.axis_index("seg")
    me = lax.axis_index("lines")
    core = lax.rem(me, 2)
    mate = me + 1 - 2 * core
    cross = me - 1 + 2 * core
    has_l = seg > 0
    has_r = seg < segs - 1
    has_x = (cross >= 0) & (cross < line_devs)

    def dev(ds, ln):
        return {"seg": seg + ds, "lines": ln}

    def line_of(u):
        return u + core * (lines - 1 - 2 * u)

    def remote(src, dst, ss, rs, where):
        return pltpu.make_async_remote_copy(
            src_ref=src, dst_ref=dst, send_sem=ss, recv_sem=rs, device_id=where, device_id_type=MESH
        )

    barrier = pltpu.get_barrier_semaphore()
    peers = []
    for ds, side in ((-1, has_l), (1, has_r)):
        peers += [(side, dev(ds, me)), (side, dev(ds, mate)), (side & has_x, dev(ds, cross))]
    peers += [(me >= 0, dev(0, mate)), (has_x, dev(0, cross))]
    for cond, where in peers:
        @pl.when(cond)
        def _():
            pl.semaphore_signal(barrier, inc=1, device_id=where, device_id_type=MESH)

    def load(u, which):
        src = (left_hbm, right_hbm)[which].at[line_of(u)]
        dst = left_v.at[u] if which == 0 else right_v.at[u, pl.ds(n, n)]
        return pltpu.make_async_copy(src, dst, load_sem.at[u, which])

    for u in range(lines):
        load(u, 0).start()
        load(u, 1).start()
    wload = pltpu.make_async_copy(w_hbm, w_v, wsem)
    wload.start()

    pl.semaphore_wait(barrier, sum(cond.astype(jnp.int32) for cond, _ in peers))

    def halo_copy(u):
        return remote(
            right_hbm.at[line_of(u)], right_v.at[u, pl.ds(0, n)], halo_ss.at[u], halo_rs.at[u],
            dev(1, me),
        )

    @pl.when(has_r)
    def _():
        for u in range(lines):
            halo_copy(u).start()

    def mt_up(u):
        return remote(own_mt.at[u], halo_in.at[u], mt_ss.at[u, 0], mt_rs.at[u, 0], dev(1, me))

    def mt_down(u):
        return remote(halo_mt.at[u], own_in.at[u], mt_ss.at[u, 1], mt_rs.at[u, 1], dev(-1, me))

    def c2_up(u):
        return remote(own_c2.at[u], halo_c2_in.at[u], c2_ss.at[u, 0], c2_rs.at[u, 0], dev(1, me))

    def c2_down(u):
        return remote(halo_c2.at[u], own_c2_in.at[u], c2_ss.at[u, 1], c2_rs.at[u, 1], dev(-1, me))

    def line_routes():
        routes = []
        for u in range(lines):
            routes.append((u, u + REACH, None, 0, me))
            if u < REACH:
                routes.append((u, REACH - 1 - u, has_x, 1, cross))
            if u >= lines - REACH:
                routes.append((u, 2 * lines + REACH - 1 - u, None, 2, mate))
        return routes

    def line_copies(u_pick):
        copies = []
        for u, slot, cond, to, ln in line_routes():
            if u_pick is not None and u != u_pick:
                continue
            mine = u + REACH
            cond = me >= 0 if cond is None else cond
            if to:
                copies.append((cond, cond, remote(
                    x0.at[mine, pl.ds(PAD, n)], x0.at[slot, pl.ds(PAD, n)],
                    ln_ss.at[u, to, 0], ln_rs.at[slot, 0], dev(0, ln))))
            copies.append((cond & has_r, cond & has_l, remote(
                x0.at[mine, pl.ds(n, PAD)], x0.at[slot, pl.ds(0, PAD)],
                ln_ss.at[u, to, 1], ln_rs.at[slot, 1], dev(1, ln))))
            copies.append((cond & has_l, cond & has_r, remote(
                x0.at[mine, pl.ds(PAD, PAD)], x0.at[slot, pl.ds(n + PAD, PAD)],
                ln_ss.at[u, to, 2], ln_rs.at[slot, 2], dev(-1, ln))))
        return copies

    e_ids = lax.broadcasted_iota(jnp.int32, (2 * n, chans), 0)
    lane = lax.broadcasted_iota(jnp.int32, (2 * n, chans), 1)
    t = n - e_ids
    low = t & 7
    tcol[...] = jnp.where(
        lane == 0, 1, jnp.where(lane == 1, t - low, jnp.where(lane == 2, low, 0))
    ).astype(F32).astype(BF16)

    @pl.when(jnp.logical_not(has_l))
    def _():
        right_v[:, 0:n, :] = jnp.zeros((lines, n, chans), BF16)
        halo_in[:, 0:1, :] = jnp.full((lines, 1, n), NEG, F32)
        halo_in[:, 1:2, :] = jnp.zeros((lines, 1, n), F32)
        halo_c2_in[...] = jnp.zeros((lines, 1, n), F32)
        x0[:, 0:PAD, :] = jnp.zeros((lines + 2 * REACH, PAD, chans), BF16)

    @pl.when(jnp.logical_not(has_r))
    def _():
        own_in[:, 0:1, :] = jnp.full((lines, 1, n), NEG, F32)
        own_in[:, 1:2, :] = jnp.zeros((lines, 1, n), F32)
        own_c2_in[...] = jnp.zeros((lines, 1, n), F32)
        x0[:, n + PAD : wide, :] = jnp.zeros((lines + 2 * REACH, PAD, chans), BF16)

    @pl.when(jnp.logical_not(has_x))
    def _():
        x0[0:REACH] = jnp.zeros((REACH, wide, chans), BF16)

    y_ref[:, 0:8, :] = jnp.zeros((6, 8, chans), F32)
    y_ref[:, 8 + wide : 16 + wide, :] = jnp.zeros((6, 8, chans), F32)

    il = lax.broadcasted_iota(jnp.int32, (blk, blk), 0)
    jl = lax.broadcasted_iota(jnp.int32, (blk, blk), 1)

    def partial_lse(u, own):
        base = n if own else 0
        dst = own_mt if own else halo_mt
        for c in range(nblk):
            cols = right_v[u, base + c * blk : base + (c + 1) * blk, :]
            run_m = jnp.full((8, blk), NEG, F32)
            run_t = jnp.zeros((8, blk), F32)
            for r in range(c, nblk) if own else range(c + 1):
                s = nt_dot(left_v[u, r * blk : (r + 1) * blk, :], cols) * scale
                if r == c:
                    s = jnp.where(jl <= il if own else jl > il, s, NEG)
                at = base + (c - r) * blk
                s_ref[u, r, :, at : at + blk] = s
                g = groups(s)
                m = jnp.maximum(run_m, jnp.max(g, axis=0))
                run_t = run_t * jnp.exp2(run_m - m) + jnp.sum(jnp.exp2(g - m[None]), axis=0)
                run_m = m
            m = jnp.max(run_m, axis=0, keepdims=True)
            dst[u, 0:1, c * blk : (c + 1) * blk] = m
            dst[u, 1:2, c * blk : (c + 1) * blk] = jnp.sum(
                run_t * jnp.exp2(run_m - m), axis=0, keepdims=True
            )

    def col_pot(a, b):
        m = jnp.maximum(a[0:1], b[0:1])
        tot = a[1:2] * jnp.exp2(a[0:1] - m) + b[1:2] * jnp.exp2(b[0:1] - m)
        return -(m + jnp.log(tot) * LOG2E)

    sub = blk // 2

    def row_pass(u):
        own = col_pot(own_mt[u], own_in[u])
        halo = jnp.where(has_l, col_pot(halo_mt[u], halo_in[u]), NEG)
        c1[:, n : 2 * n] = jnp.broadcast_to(own, (8, n))
        c1[:, 0:n] = jnp.broadcast_to(halo, (8, n))
        c2acc[...] = jnp.zeros((8, 2 * n), F32)

        def step(k, carry):
            r = k // 2
            rows = pl.multiple_of(lax.rem(k, 2) * sub, sub)
            at = pl.multiple_of(r * blk, blk)
            pot = c1[:, pl.ds(at, win)][None]
            total = jnp.zeros((8, win), F32)
            piece = sub // 4
            for p in range(4):
                here = pl.ds(rows + p * piece, piece)
                sc = groups(s_ref[u, r, here, :]) + pot
                k_el = jnp.exp2(sc - jnp.max(sc, axis=2, keepdims=True))
                s_ref[u, r, here, :] = k_el.reshape(piece, win)
                inv = 1.0 / jnp.sum(k_el, axis=2, keepdims=True)
                total = total + jnp.sum(k_el * inv, axis=0)
            c2acc[:, pl.ds(at, win)] += total
            return carry

        lax.fori_loop(0, 2 * nblk, step, 0)
        halo_c2[u] = jnp.sum(c2acc[:, 0:n], axis=0, keepdims=True)
        own_c2[u] = jnp.sum(c2acc[:, n : 2 * n], axis=0, keepdims=True)

    def transport(u):
        c1[:, n : 2 * n] = jnp.broadcast_to(1.0 / (own_c2[u] + own_c2_in[u]), (8, n))
        c1[:, 0:n] = jnp.broadcast_to(
            jnp.where(has_l, 1.0 / (halo_c2[u] + halo_c2_in[u]), 0.0), (8, n)
        )
        ln = line_of(u)

        def step(r, carry):
            at = pl.multiple_of(r * blk, blk)
            q = groups(s_ref[u, r]) * c1[:, pl.ds(at, win)][None]
            q = q.reshape(blk, win).astype(BF16)
            rhs = jnp.concatenate([right_v[u, pl.ds(at, win), :], tcol[pl.ds(at, win), :]], axis=1)
            o = jnp.dot(q, rhs, preferred_element_type=F32)
            matched = o[:, :chans] / o[:, chans : chans + 1]
            x0[u + REACH, pl.ds(PAD + at, blk), :] = (
                matched - left_v[u, pl.ds(at, blk), :].astype(F32)
            ).astype(BF16)
            rowed = jnp.transpose(o[:, chans:])
            ids = (lax.broadcasted_iota(jnp.int32, (1, blk), 1) + at).astype(F32)
            disp_ref[pl.ds(ln, 1), pl.ds(at, blk)] = ids + (rowed[1:2] + rowed[2:3]) / rowed[0:1]
            return carry

        lax.fori_loop(0, nblk, step, 0)

    def own_step(u, carry):
        load(u, 0).wait()
        load(u, 1).wait()
        partial_lse(u, True)

        @pl.when(has_r)
        def _():
            mt_up(u).start()

        return carry

    lax.fori_loop(0, lines, own_step, 0)

    wload.wait()
    wbig[...] = jnp.zeros(wbig.shape, BF16)
    for k in range(layers):
        for a in range(3):
            tap = a + core * (2 - 2 * a)
            for b in range(3):
                w = w_v[k, tap, b]
                for h in range(2):
                    wbig[k, (a + h) * chans : (a + h + 1) * chans,
                         (3 * h + b) * chans : (3 * h + b + 1) * chans] = w

    for u in range(lines + 1):
        if u < lines:
            @pl.when(has_l)
            def _():
                halo_copy(u).wait_recv()

            partial_lse(u, False)

            @pl.when(has_l)
            def _():
                mt_down(u).start()

        if u > 0:
            @pl.when(has_l)
            def _():
                c2_up(u - 1).wait_recv()

            @pl.when(has_r)
            def _():
                c2_down(u - 1).wait_recv()

            transport(u - 1)
            for cond, _, copy in line_copies(u - 1):
                @pl.when(cond)
                def _():
                    copy.start()

        if u < lines:
            @pl.when(has_l)
            def _():
                mt_up(u).wait_recv()

            @pl.when(has_r)
            def _():
                mt_down(u).wait_recv()

            row_pass(u)

            @pl.when(has_r)
            def _():
                c2_up(u).start()

            @pl.when(has_l)
            def _():
                c2_down(u).start()

    for _, cond, copy in line_copies(None):
        @pl.when(cond)
        def _():
            copy.wait_recv()

    part = wide // 3 if (wide // 3) % 16 == 0 else wide
    step_rows = 96

    def conv_pair(src, k, slot, store):
        for g in range(wide // part):
            rows = slice(g * part, (g + 1) * part)
            ins = jnp.concatenate([src[slot - 1 + i, rows, :] for i in range(4)], axis=1)
            y = jnp.dot(ins, wbig[k], preferred_element_type=F32)
            for j in range(6):
                y_ref[j, 8 + g * part : 8 + (g + 1) * part, :] = y[:, j * chans : (j + 1) * chans]
        for h in range(2):
            store(h, src, slot + h, bias_ref[k : k + 1, :])

    def updated(h, src, slot, bias, at, rows):
        total = (
            y_ref[3 * h, 7 + at : 7 + at + rows, :]
            + y_ref[3 * h + 1, 8 + at : 8 + at + rows, :]
            + y_ref[3 * h + 2, 9 + at : 9 + at + rows, :]
        )
        state = src[slot, at : at + rows, :].astype(F32)
        return (state + jnp.maximum(total + bias, 0.0)).astype(BF16)

    def layer(src, dst, k, first, last):
        def keep(h, src, slot, bias):
            for at in range(0, wide, step_rows):
                dst[slot, at : at + step_rows, :] = updated(h, src, slot, bias, at, step_rows)

        for slot in range(first, last, 2):
            conv_pair(src, k, slot, keep)

        @pl.when(jnp.logical_not(has_l))
        def _():
            dst[first:last, 0:PAD, :] = jnp.zeros((last - first, PAD, chans), BF16)

        @pl.when(jnp.logical_not(has_r))
        def _():
            dst[first:last, n + PAD : wide, :] = jnp.zeros((last - first, PAD, chans), BF16)

        @pl.when(jnp.logical_not(has_x))
        def _():
            dst[first:REACH] = jnp.zeros((REACH - first, wide, chans), BF16)

    layer(x0, x1, 0, 1, lines + 5)
    layer(x1, x2, 1, 2, lines + 4)

    def put(h, src, slot, bias):
        ln = line_of(slot - REACH)
        for at in range(0, n, 128):
            out_ref[ln, at : at + 128, :] = updated(h, src, slot, bias, at + PAD, 128)

    for slot in range(REACH, REACH + lines, 2):
        conv_pair(x2, 2, slot, put)

    @pl.when(has_r)
    def _():
        for u in range(lines):
            halo_copy(u).wait_send()
            mt_up(u).wait_send()
            c2_up(u).wait_send()

    @pl.when(has_l)
    def _():
        for u in range(lines):
            mt_down(u).wait_send()
            c2_down(u).wait_send()

    for cond, _, copy in line_copies(None):
        @pl.when(cond)
        def _():
            copy.wait_send()


def shards(segs, line_devs, left, right, weight, bias):
    lines, n, chans = left.shape
    layers = weight.shape[0]
    blk = n // 4
    wide = n + 2 * PAD
    slots = lines + 2 * REACH
    shape = (segs, line_devs, lines, n, blk, chans, layers)
    dma = pltpu.SemaphoreType.DMA
    vm = pltpu.VMEM
    return pl.pallas_call(
        functools.partial(body, shape),
        out_shape=(
            jax.ShapeDtypeStruct((lines, n, chans), BF16),
            jax.ShapeDtypeStruct((lines, n), F32),
        ),
        in_specs=[pl.BlockSpec(memory_space=pl.ANY)] * 3 + [pl.BlockSpec(memory_space=vm)],
        out_specs=(pl.BlockSpec(memory_space=vm), pl.BlockSpec(memory_space=vm)),
        scratch_shapes=[
            vm((lines, n, chans), BF16),
            vm((lines, 2 * n, chans), BF16),
            vm((2 * n, chans), BF16),
            vm((lines, 4, blk, n + blk), F32),
            vm((lines, 2, n), F32),
            vm((lines, 2, n), F32),
            vm((lines, 2, n), F32),
            vm((lines, 2, n), F32),
            vm((8, 2 * n), F32),
            vm((8, 2 * n), F32),
            vm((lines, 1, n), F32),
            vm((lines, 1, n), F32),
            vm((lines, 1, n), F32),
            vm((lines, 1, n), F32),
            vm(weight.shape, BF16),
            vm((layers, 4 * chans, 6 * chans), BF16),
            vm((slots, wide, chans), BF16),
            vm((slots, wide, chans), BF16),
            vm((slots, wide, chans), BF16),
            vm((6, wide + 16, chans), F32),
            dma((lines, 2)),
            dma,
            dma((lines,)),
            dma((lines,)),
            dma((lines, 2)),
            dma((lines, 2)),
            dma((lines, 2)),
            dma((lines, 2)),
            dma((lines, 3, 3)),
            dma((slots, 3)),
        ],
        compiler_params=pltpu.CompilerParams(
            collective_id=0, has_side_effects=True, vmem_limit_bytes=60 * 1024 * 1024
        ),
        name="stereo",
    )(left, right, weight, bias)


def solution(mesh):
    return jax.shard_map(
        functools.partial(shards, mesh.shape["seg"], mesh.shape["lines"]),
        mesh=mesh,
        in_specs=(P("lines", "seg", None), P("lines", "seg", None), P(), P()),
        out_specs=(P("lines", "seg", None), P("lines", "seg")),
        check_vma=False,
    )
```

profile of v0, /device:TPU:7, one launch (start us, length us, event | category | flops | bytes accessed | tf_op | source)
XLA Modules:
  0.0 90.7 jit_solution(12892454930236850248)
XLA Ops:
  0.6 87.1 %stereo.1 = (bf16[4,1024,128]{2,1,0:T(8,128)(2,1)}, f32[4,1024]{1,0:T(4,128)}) custom-call(bf16[4,1024,128]{2,1,0:T(8,128)(2,1)} %left_hbm.1, bf16[4,1024,128]{2,1,0:T(8,128)(2,1)} %right_hbm.1, bf16[3,3,3,128,128]{4,3,2,1,0:T(8,128)(2,1)} %w_hbm.1, f32[3,128]{1,0:T(4,128)} %bias_ref.1), custom_call_target="tpu_custom_call" | custom-call | tf_op jit(solution)/shard_map/stereo/pallas_call | solution.py:405
  87.8 0.0 copy-start
  87.8 2.3 %copy.8 = bf16[4,1024,128]{2,1,0:T(8,128)(2,1)} copy(bf16[4,1024,128]{2,1,0:T(8,128)(2,1)} %get-tuple-element.4) | data formatting | bytes 2097152
  90.1 0.0 copy-done
  90.1 0.6 copy.9
Async XLA Ops:
  87.8 2.3 %copy-start = (f32[4,1024]{1,0:T(4,128)S(1)}, f32[4,1024]{1,0:T(4,128)}, u32[]{:S(2)}) copy-start(f32[4,1024]{1,0:T(4,128)} %get-tuple-element.5) | copy-start | bytes 49156
where the time goes:
time: 91.5 us; the launch traced here: 90.7 us
  Pallas kernels  87.1 us (95%)
  local copies, waits for them, and re-layouts  2.88 us (3%)
    pallas_call x1, Pallas kernels, shards(): pl.pallas_call(functools.partial(body, shape), out_shape=(jax.ShapeDtypeS...  87.1 us
    unnamed x4, local copies, waits for them, and re-layouts  2.88 us

commit v1 on v0

--- a/solution.py
+++ b/solution.py
@@ -27,7 +27,7 @@
 
 def body(
     shape, left_hbm, right_hbm, w_hbm, bias_ref, out_ref, disp_ref,
-    left_v, right_v, tcol, s_ref, own_mt, halo_mt, own_in, halo_in, c1, c2acc,
+    left_v, right_v, tcol, s_ref, rm_ref, iv_ref, own_mt, halo_mt, own_in, halo_in, c1, c2acc,
     own_c2, halo_c2, own_c2_in, halo_c2_in, w_v, wbig, x0, x1, x2, y_ref,
     load_sem, wsem, halo_ss, halo_rs, mt_ss, mt_rs, c2_ss, c2_rs, ln_ss, ln_rs,
 ):
@@ -85,10 +85,12 @@
             dev(1, me),
         )
 
-    @pl.when(has_r)
-    def _():
-        for u in range(lines):
+    def send_halo(u):
+        @pl.when(has_r)
+        def _():
             halo_copy(u).start()
+
+    send_halo(0)
 
     def mt_up(u):
         return remote(own_mt.at[u], halo_in.at[u], mt_ss.at[u, 0], mt_rs.at[u, 0], dev(1, me))
@@ -112,10 +114,10 @@
                 routes.append((u, 2 * lines + REACH - 1 - u, None, 2, mate))
         return routes
 
-    def line_copies(u_pick):
+    def line_copies(u_pick, slots=None):
         copies = []
         for u, slot, cond, to, ln in line_routes():
-            if u_pick is not None and u != u_pick:
+            if u_pick is not None and u != u_pick or slots is not None and slot not in slots:
                 continue
             mine = u + REACH
             cond = me >= 0 if cond is None else cond
@@ -176,7 +178,7 @@
                 if r == c:
                     s = jnp.where(jl <= il if own else jl > il, s, NEG)
                 at = base + (c - r) * blk
-                s_ref[u, r, :, at : at + blk] = s
+                s_ref[u, r * blk : (r + 1) * blk, at : at + blk] = s
                 g = groups(s)
                 m = jnp.maximum(run_m, jnp.max(g, axis=0))
                 run_t = run_t * jnp.exp2(run_m - m) + jnp.sum(jnp.exp2(g - m[None]), axis=0)
@@ -192,7 +194,50 @@
         tot = a[1:2] * jnp.exp2(a[0:1] - m) + b[1:2] * jnp.exp2(b[0:1] - m)
         return -(m + jnp.log(tot) * LOG2E)
 
-    sub = blk // 2
+    rows_at = min(64, blk)
+    steps = n // rows_at
+    tiles = [slice(j * 128, min(win, (j + 1) * 128)) for j in range(-(-win // 128))]
+
+    def pot_at(k):
+        return pl.multiple_of((k * rows_at) // blk * blk, blk)
+
+    def row_max(u, k):
+        here = pl.ds(pl.multiple_of(k * rows_at, rows_at), rows_at)
+        top = None
+        for tile in tiles:
+            width = tile.stop - tile.start
+            pot = c1[:, pl.ds(pot_at(k) + tile.start, width)]
+            t = groups(s_ref[u, here, tile]) + pot[None]
+            s_ref[u, here, tile] = t.reshape(rows_at, width)
+            if width < 128:
+                t = jnp.concatenate([t] * (128 // width), axis=2)
+            top = t if top is None else jnp.maximum(top, t)
+        top = jnp.max(top, axis=2, keepdims=True)
+        rm_ref[here, :] = jnp.broadcast_to(top, (rows_at // 8, 8, chans)).reshape(rows_at, chans)
+
+    def row_exp(u, k):
+        here = pl.ds(pl.multiple_of(k * rows_at, rows_at), rows_at)
+        top = groups(rm_ref[here, :])
+        total = jnp.zeros((rows_at // 8, 8, 1), F32)
+        acc = None
+        for tile in tiles:
+            width = tile.stop - tile.start
+            e = jnp.exp2(groups(s_ref[u, here, tile]) - top[:, :, :width])
+            s_ref[u, here, tile] = e.reshape(rows_at, width)
+            if width < 128:
+                total = total + jnp.sum(e, axis=2, keepdims=True)
+            else:
+                acc = e if acc is None else acc + e
+        inv = 1.0 / (total + jnp.sum(acc, axis=2, keepdims=True))
+        iv_ref[here, :] = jnp.broadcast_to(inv, (rows_at // 8, 8, chans)).reshape(rows_at, chans)
+
+    def col_sum(u, k):
+        here = pl.ds(pl.multiple_of(k * rows_at, rows_at), rows_at)
+        inv = groups(iv_ref[here, :])
+        for tile in tiles:
+            width = tile.stop - tile.start
+            part = jnp.sum(groups(s_ref[u, here, tile]) * inv[:, :, :width], axis=0)
+            c2acc[:, pl.ds(pot_at(k) + tile.start, width)] += part
 
     def row_pass(u):
         own = col_pot(own_mt[u], own_in[u])
@@ -200,25 +245,20 @@
         c1[:, n : 2 * n] = jnp.broadcast_to(own, (8, n))
         c1[:, 0:n] = jnp.broadcast_to(halo, (8, n))
         c2acc[...] = jnp.zeros((8, 2 * n), F32)
+        row_max(u, 0)
+        row_exp(u, 0)
+        row_max(u, 1)
 
         def step(k, carry):
-            r = k // 2
-            rows = pl.multiple_of(lax.rem(k, 2) * sub, sub)
-            at = pl.multiple_of(r * blk, blk)
-            pot = c1[:, pl.ds(at, win)][None]
-            total = jnp.zeros((8, win), F32)
-            piece = sub // 4
-            for p in range(4):
-                here = pl.ds(rows + p * piece, piece)
-                sc = groups(s_ref[u, r, here, :]) + pot
-                k_el = jnp.exp2(sc - jnp.max(sc, axis=2, keepdims=True))
-                s_ref[u, r, here, :] = k_el.reshape(piece, win)
-                inv = 1.0 / jnp.sum(k_el, axis=2, keepdims=True)
-                total = total + jnp.sum(k_el * inv, axis=0)
-            c2acc[:, pl.ds(at, win)] += total
+            col_sum(u, k - 2)
+            row_max(u, k)
+            row_exp(u, k - 1)
             return carry
 
-        lax.fori_loop(0, 2 * nblk, step, 0)
+        lax.fori_loop(2, steps, step, 0)
+        col_sum(u, steps - 2)
+        row_exp(u, steps - 1)
+        col_sum(u, steps - 1)
         halo_c2[u] = jnp.sum(c2acc[:, 0:n], axis=0, keepdims=True)
         own_c2[u] = jnp.sum(c2acc[:, n : 2 * n], axis=0, keepdims=True)
 
@@ -231,7 +271,7 @@
 
         def step(r, carry):
             at = pl.multiple_of(r * blk, blk)
-            q = groups(s_ref[u, r]) * c1[:, pl.ds(at, win)][None]
+            q = groups(s_ref[u, pl.ds(at, blk), :]) * c1[:, pl.ds(at, win)][None]
             q = q.reshape(blk, win).astype(BF16)
             rhs = jnp.concatenate([right_v[u, pl.ds(at, win), :], tcol[pl.ds(at, win), :]], axis=1)
             o = jnp.dot(q, rhs, preferred_element_type=F32)
@@ -258,6 +298,7 @@
         return carry
 
     lax.fori_loop(0, lines, own_step, 0)
+    send_halo(1)
 
     wload.wait()
     wbig[...] = jnp.zeros(wbig.shape, BF16)
@@ -270,56 +311,56 @@
                     wbig[k, (a + h) * chans : (a + h + 1) * chans,
                          (3 * h + b) * chans : (3 * h + b + 1) * chans] = w
 
-    for u in range(lines + 1):
-        if u < lines:
-            @pl.when(has_l)
+    def scores_step(u):
+        @pl.when(has_l)
+        def _():
+            halo_copy(u).wait_recv()
+
+        partial_lse(u, False)
+
+        @pl.when(has_l)
+        def _():
+            mt_down(u).start()
+
+    def row_step(u):
+        @pl.when(has_l)
+        def _():
+            mt_up(u).wait_recv()
+
+        @pl.when(has_r)
+        def _():
+            mt_down(u).wait_recv()
+
+        row_pass(u)
+
+        @pl.when(has_r)
+        def _():
+            c2_up(u).start()
+
+        @pl.when(has_l)
+        def _():
+            c2_down(u).start()
+
+    def plan_step(u):
+        @pl.when(has_l)
+        def _():
+            c2_up(u).wait_recv()
+
+        @pl.when(has_r)
+        def _():
+            c2_down(u).wait_recv()
+
+        transport(u)
+        for cond, _, copy in line_copies(u):
+            @pl.when(cond)
             def _():
-                halo_copy(u).wait_recv()
-
-            partial_lse(u, False)
-
-            @pl.when(has_l)
+                copy.start()
+
+    def wait_slots(slots):
+        for _, cond, copy in line_copies(None, slots):
+            @pl.when(cond)
             def _():
-                mt_down(u).start()
-
-        if u > 0:
-            @pl.when(has_l)
-            def _():
-                c2_up(u - 1).wait_recv()
-
-            @pl.when(has_r)
-            def _():
-                c2_down(u - 1).wait_recv()
-
-            transport(u - 1)
-            for cond, _, copy in line_copies(u - 1):
-                @pl.when(cond)
-                def _():
-                    copy.start()
-
-        if u < lines:
-            @pl.when(has_l)
-            def _():
-                mt_up(u).wait_recv()
-
-            @pl.when(has_r)
-            def _():
-                mt_down(u).wait_recv()
-
-            row_pass(u)
-
-            @pl.when(has_r)
-            def _():
-                c2_up(u).start()
-
-            @pl.when(has_l)
-            def _():
-                c2_down(u).start()
-
-    for _, cond, copy in line_copies(None):
-        @pl.when(cond)
-        def _():
-            copy.wait_recv()
+                copy.wait_recv()
 
     part = wide // 3 if (wide // 3) % 16 == 0 else wide
     step_rows = 96
@@ -343,36 +384,58 @@
         state = src[slot, at : at + rows, :].astype(F32)
         return (state + jnp.maximum(total + bias, 0.0)).astype(BF16)
 
-    def layer(src, dst, k, first, last):
+    def clear_edges(dst, first, last):
+        @pl.when(jnp.logical_not(has_l))
+        def _():
+            dst[first:last, 0:PAD, :] = jnp.zeros((last - first, PAD, chans), BF16)
+
+        @pl.when(jnp.logical_not(has_r))
+        def _():
+            dst[first:last, n + PAD : wide, :] = jnp.zeros((last - first, PAD, chans), BF16)
+
+        if first < REACH:
+            stop = min(last, REACH)
+
+            @pl.when(jnp.logical_not(has_x))
+            def _():
+                dst[first:stop] = jnp.zeros((stop - first, wide, chans), BF16)
+
+    def layer_pair(src, dst, k, first):
         def keep(h, src, slot, bias):
             for at in range(0, wide, step_rows):
                 dst[slot, at : at + step_rows, :] = updated(h, src, slot, bias, at, step_rows)
 
-        for slot in range(first, last, 2):
-            conv_pair(src, k, slot, keep)
-
-        @pl.when(jnp.logical_not(has_l))
-        def _():
-            dst[first:last, 0:PAD, :] = jnp.zeros((last - first, PAD, chans), BF16)
-
-        @pl.when(jnp.logical_not(has_r))
-        def _():
-            dst[first:last, n + PAD : wide, :] = jnp.zeros((last - first, PAD, chans), BF16)
-
-        @pl.when(jnp.logical_not(has_x))
-        def _():
-            dst[first:REACH] = jnp.zeros((REACH - first, wide, chans), BF16)
-
-    layer(x0, x1, 0, 1, lines + 5)
-    layer(x1, x2, 1, 2, lines + 4)
+        conv_pair(src, k, first, keep)
+        clear_edges(dst, first, first + 2)
 
     def put(h, src, slot, bias):
         ln = line_of(slot - REACH)
         for at in range(0, n, 128):
             out_ref[ln, at : at + 128, :] = updated(h, src, slot, bias, at + PAD, 128)
 
-    for slot in range(REACH, REACH + lines, 2):
-        conv_pair(x2, 2, slot, put)
+    for u in range(lines):
+        scores_step(u)
+        if u >= 1:
+            row_step(u - 1)
+        if u + 2 < lines:
+            send_halo(u + 2)
+        if u >= 2:
+            plan_step(u - 2)
+    row_step(lines - 1)
+    plan_step(lines - 2)
+    wait_slots((2, 3, 4, 5))
+    layer_pair(x0, x1, 0, 3)
+    plan_step(lines - 1)
+    wait_slots((0, 1))
+    layer_pair(x0, x1, 0, 1)
+    layer_pair(x1, x2, 1, 2)
+    wait_slots((6, 7, 8, 9))
+    layer_pair(x0, x1, 0, 5)
+    layer_pair(x0, x1, 0, 7)
+    layer_pair(x1, x2, 1, 4)
+    layer_pair(x1, x2, 1, 6)
+    conv_pair(x2, 2, 3, put)
+    conv_pair(x2, 2, 5, put)
 
     @pl.when(has_r)
     def _():
@@ -414,7 +477,9 @@
             vm((lines, n, chans), BF16),
             vm((lines, 2 * n, chans), BF16),
             vm((2 * n, chans), BF16),
-            vm((lines, 4, blk, n + blk), F32),
+            vm((lines, n, n + blk), F32),
+            vm((n, chans), F32),
+            vm((n, chans), F32),
             vm((lines, 2, n), F32),
             vm((lines, 2, n), F32),
             vm((lines, 2, n), F32),

time: 91.5 us -> 71.8 us (0.78)
  Pallas kernels: 87.1 us -> 67 us
    pallas_call x1, Pallas kernels: 87.1 us -> 67 us  [shards(): pl.pallas_call(functools.partial(body, shape), out_shape=(jax.ShapeDtypeS...]
where the time goes in v1:
time: 71.8 us; the launch traced here: 70.5 us
  Pallas kernels  67 us (93%)
  local copies, waits for them, and re-layouts  2.88 us (4%)
    pallas_call x1, Pallas kernels, shards(): pl.pallas_call(functools.partial(body, shape), out_shape=(jax.ShapeDtypeS...  67 us
    unnamed x4, local copies, waits for them, and re-layouts  2.88 us

profile of v1, /device:TPU:7, one launch (start us, length us, event | category | flops | bytes accessed | tf_op | source)
XLA Modules:
  0.0 70.5 jit_solution(16330788893824001595)
XLA Ops:
  0.6 67.0 %stereo.1 = (bf16[4,1024,128]{2,1,0:T(8,128)(2,1)}, f32[4,1024]{1,0:T(4,128)}) custom-call(bf16[4,1024,128]{2,1,0:T(8,128)(2,1)} %left_hbm.1, bf16[4,1024,128]{2,1,0:T(8,128)(2,1)} %right_hbm.1, bf16[3,3,3,128,128]{4,3,2,1,0:T(8,128)(2,1)} %w_hbm.1, f32[3,128]{1,0:T(4,128)} %bias_ref.1), custom_call_target="tpu_custom_call" | custom-call | tf_op jit(solution)/shard_map/stereo/pallas_call | solution.py:468
  67.6 0.0 copy-start
  67.6 2.3 %copy.8 = bf16[4,1024,128]{2,1,0:T(8,128)(2,1)} copy(bf16[4,1024,128]{2,1,0:T(8,128)(2,1)} %get-tuple-element.4) | data formatting | bytes 2097152
  69.9 0.0 copy-done
  69.9 0.6 copy.9
Async XLA Ops:
  67.6 2.3 %copy-start = (f32[4,1024]{1,0:T(4,128)S(1)}, f32[4,1024]{1,0:T(4,128)}, u32[]{:S(2)}) copy-start(f32[4,1024]{1,0:T(4,128)} %get-tuple-element.5) | copy-start | bytes 49156

commit v2 on v1

--- a/solution.py
+++ b/solution.py
@@ -27,7 +27,7 @@
 
 def body(
     shape, left_hbm, right_hbm, w_hbm, bias_ref, out_ref, disp_ref,
-    left_v, right_v, tcol, s_ref, rm_ref, iv_ref, own_mt, halo_mt, own_in, halo_in, c1, c2acc,
+    left_v, right_v, tcol, s_ref, k_ref, own_mt, halo_mt, own_in, halo_in, c1, c2acc,
     own_c2, halo_c2, own_c2_in, halo_c2_in, w_v, wbig, x0, x1, x2, y_ref,
     load_sem, wsem, halo_ss, halo_rs, mt_ss, mt_rs, c2_ss, c2_rs, ln_ss, ln_rs,
 ):
@@ -163,30 +163,35 @@
     y_ref[:, 0:8, :] = jnp.zeros((6, 8, chans), F32)
     y_ref[:, 8 + wide : 16 + wide, :] = jnp.zeros((6, 8, chans), F32)
 
-    il = lax.broadcasted_iota(jnp.int32, (blk, blk), 0)
-    jl = lax.broadcasted_iota(jnp.int32, (blk, blk), 1)
+    il = lax.broadcasted_iota(jnp.int32, (blk // 2, blk), 0)
+    jl = lax.broadcasted_iota(jnp.int32, (blk // 2, blk), 1)
 
     def partial_lse(u, own):
         base = n if own else 0
         dst = own_mt if own else halo_mt
         for c in range(nblk):
             cols = right_v[u, base + c * blk : base + (c + 1) * blk, :]
-            run_m = jnp.full((8, blk), NEG, F32)
-            run_t = jnp.zeros((8, blk), F32)
+            pieces = []
+            top = jnp.full((8, blk), NEG, F32)
             for r in range(c, nblk) if own else range(c + 1):
-                s = nt_dot(left_v[u, r * blk : (r + 1) * blk, :], cols) * scale
-                if r == c:
-                    s = jnp.where(jl <= il if own else jl > il, s, NEG)
                 at = base + (c - r) * blk
-                s_ref[u, r * blk : (r + 1) * blk, at : at + blk] = s
-                g = groups(s)
-                m = jnp.maximum(run_m, jnp.max(g, axis=0))
-                run_t = run_t * jnp.exp2(run_m - m) + jnp.sum(jnp.exp2(g - m[None]), axis=0)
-                run_m = m
-            m = jnp.max(run_m, axis=0, keepdims=True)
+                for h in range(2):
+                    rows = slice(r * blk + h * (blk // 2), r * blk + (h + 1) * (blk // 2))
+                    s = nt_dot(left_v[u, rows, :], cols) * scale
+                    if r == c:
+                        ih = il + h * (blk // 2)
+                        s = jnp.where(jl <= ih if own else jl > ih, s, NEG)
+                    s_ref[u, rows, at : at + blk] = s
+                    top = jnp.maximum(top, jnp.max(groups(s), axis=0))
+                    pieces.append((rows, at))
+            total = jnp.zeros((8, blk), F32)
+            for rows, at in pieces:
+                g = groups(s_ref[u, rows, at : at + blk])
+                total = total + jnp.sum(jnp.exp2(g - top[None]), axis=0)
+            m = jnp.max(top, axis=0, keepdims=True)
             dst[u, 0:1, c * blk : (c + 1) * blk] = m
             dst[u, 1:2, c * blk : (c + 1) * blk] = jnp.sum(
-                run_t * jnp.exp2(run_m - m), axis=0, keepdims=True
+                total * jnp.exp2(top - m), axis=0, keepdims=True
             )
 
     def col_pot(a, b):
@@ -208,35 +213,30 @@
             width = tile.stop - tile.start
             pot = c1[:, pl.ds(pot_at(k) + tile.start, width)]
             t = groups(s_ref[u, here, tile]) + pot[None]
-            s_ref[u, here, tile] = t.reshape(rows_at, width)
             if width < 128:
                 t = jnp.concatenate([t] * (128 // width), axis=2)
             top = t if top is None else jnp.maximum(top, t)
-        top = jnp.max(top, axis=2, keepdims=True)
-        rm_ref[here, :] = jnp.broadcast_to(top, (rows_at // 8, 8, chans)).reshape(rows_at, chans)
-
-    def row_exp(u, k):
+        return jnp.broadcast_to(jnp.max(top, axis=2, keepdims=True), top.shape)
+
+    def row_exp(u, k, top):
         here = pl.ds(pl.multiple_of(k * rows_at, rows_at), rows_at)
-        top = groups(rm_ref[here, :])
-        total = jnp.zeros((rows_at // 8, 8, 1), F32)
-        acc = None
+        total = None
         for tile in tiles:
             width = tile.stop - tile.start
-            e = jnp.exp2(groups(s_ref[u, here, tile]) - top[:, :, :width])
-            s_ref[u, here, tile] = e.reshape(rows_at, width)
+            pot = c1[:, pl.ds(pot_at(k) + tile.start, width)]
+            t = groups(s_ref[u, here, tile]) + pot[None]
+            e = jnp.exp2(t - top[:, :, :width])
+            k_ref[u % 2, here, tile] = e.reshape(rows_at, width)
             if width < 128:
-                total = total + jnp.sum(e, axis=2, keepdims=True)
-            else:
-                acc = e if acc is None else acc + e
-        inv = 1.0 / (total + jnp.sum(acc, axis=2, keepdims=True))
-        iv_ref[here, :] = jnp.broadcast_to(inv, (rows_at // 8, 8, chans)).reshape(rows_at, chans)
-
-    def col_sum(u, k):
+                e = jnp.concatenate([e, jnp.zeros(e.shape[:2] + (128 - width,), F32)], axis=2)
+            total = e if total is None else total + e
+        return jnp.broadcast_to(1.0 / jnp.sum(total, axis=2, keepdims=True), total.shape)
+
+    def col_sum(u, k, inv):
         here = pl.ds(pl.multiple_of(k * rows_at, rows_at), rows_at)
-        inv = groups(iv_ref[here, :])
         for tile in tiles:
             width = tile.stop - tile.start
-            part = jnp.sum(groups(s_ref[u, here, tile]) * inv[:, :, :width], axis=0)
+            part = jnp.sum(groups(k_ref[u % 2, here, tile]) * inv[:, :, :width], axis=0)
             c2acc[:, pl.ds(pot_at(k) + tile.start, width)] += part
 
     def row_pass(u):
@@ -245,20 +245,18 @@
         c1[:, n : 2 * n] = jnp.broadcast_to(own, (8, n))
         c1[:, 0:n] = jnp.broadcast_to(halo, (8, n))
         c2acc[...] = jnp.zeros((8, 2 * n), F32)
-        row_max(u, 0)
-        row_exp(u, 0)
-        row_max(u, 1)
+        inv = row_exp(u, 0, row_max(u, 0))
+        top = row_max(u, 1)
 
         def step(k, carry):
-            col_sum(u, k - 2)
-            row_max(u, k)
-            row_exp(u, k - 1)
-            return carry
-
-        lax.fori_loop(2, steps, step, 0)
-        col_sum(u, steps - 2)
-        row_exp(u, steps - 1)
-        col_sum(u, steps - 1)
+            top, inv = carry
+            col_sum(u, k - 2, inv)
+            inv = row_exp(u, k - 1, top)
+            return row_max(u, k), inv
+
+        top, inv = lax.fori_loop(2, steps, step, (top, inv))
+        col_sum(u, steps - 2, inv)
+        col_sum(u, steps - 1, row_exp(u, steps - 1, top))
         halo_c2[u] = jnp.sum(c2acc[:, 0:n], axis=0, keepdims=True)
         own_c2[u] = jnp.sum(c2acc[:, n : 2 * n], axis=0, keepdims=True)
 
@@ -269,22 +267,18 @@
         )
         ln = line_of(u)
 
-        def step(r, carry):
-            at = pl.multiple_of(r * blk, blk)
-            q = groups(s_ref[u, pl.ds(at, blk), :]) * c1[:, pl.ds(at, win)][None]
+        for at in range(0, n, blk):
+            q = groups(k_ref[u % 2, pl.ds(at, blk), :]) * c1[:, pl.ds(at, win)][None]
             q = q.reshape(blk, win).astype(BF16)
             rhs = jnp.concatenate([right_v[u, pl.ds(at, win), :], tcol[pl.ds(at, win), :]], axis=1)
             o = jnp.dot(q, rhs, preferred_element_type=F32)
-            matched = o[:, :chans] / o[:, chans : chans + 1]
+            matched = o[:, :chans] * (1.0 / o[:, chans : chans + 1])
             x0[u + REACH, pl.ds(PAD + at, blk), :] = (
                 matched - left_v[u, pl.ds(at, blk), :].astype(F32)
             ).astype(BF16)
             rowed = jnp.transpose(o[:, chans:])
             ids = (lax.broadcasted_iota(jnp.int32, (1, blk), 1) + at).astype(F32)
             disp_ref[pl.ds(ln, 1), pl.ds(at, blk)] = ids + (rowed[1:2] + rowed[2:3]) / rowed[0:1]
-            return carry
-
-        lax.fori_loop(0, nblk, step, 0)
 
     def own_step(u, carry):
         load(u, 0).wait()
@@ -478,8 +472,7 @@
             vm((lines, 2 * n, chans), BF16),
             vm((2 * n, chans), BF16),
             vm((lines, n, n + blk), F32),
-            vm((n, chans), F32),
-            vm((n, chans), F32),
+            vm((2, n, n + blk), F32),
             vm((lines, 2, n), F32),
             vm((lines, 2, n), F32),
             vm((lines, 2, n), F32),

time: 71.8 us -> 65.6 us (0.914); the launches traced: 70.5 us -> 65.4 us
  Pallas kernels: 67 us -> 61.9 us
    pallas_call x1, Pallas kernels: 67 us -> 61.9 us  [shards(): pl.pallas_call(functools.partial(body, shape), out_shape=(jax.ShapeDtypeS...]
where the time goes in v2:
time: 65.6 us; the launch traced here: 65.4 us
  Pallas kernels  61.9 us (94%)
  local copies, waits for them, and re-layouts  2.88 us (4%)
    pallas_call x1, Pallas kernels, shards(): pl.pallas_call(functools.partial(body, shape), out_shape=(jax.ShapeDtypeS...  61.9 us
    unnamed x4, local copies, waits for them, and re-layouts  2.88 us

profile of v2, /device:TPU:7, one launch (start us, length us, event | category | flops | bytes accessed | tf_op | source)
XLA Modules:
  0.0 65.4 jit_solution(5479551747162576503)
XLA Ops:
  0.6 61.9 %stereo.1 = (bf16[4,1024,128]{2,1,0:T(8,128)(2,1)}, f32[4,1024]{1,0:T(4,128)}) custom-call(bf16[4,1024,128]{2,1,0:T(8,128)(2,1)} %left_hbm.1, bf16[4,1024,128]{2,1,0:T(8,128)(2,1)} %right_hbm.1, bf16[3,3,3,128,128]{4,3,2,1,0:T(8,128)(2,1)} %w_hbm.1, f32[3,128]{1,0:T(4,128)} %bias_ref.1), custom_call_target="tpu_custom_call" | custom-call | tf_op jit(solution)/shard_map/stereo/pallas_call | solution.py:462
  62.5 0.0 copy-start
  62.6 2.3 %copy.8 = bf16[4,1024,128]{2,1,0:T(8,128)(2,1)} copy(bf16[4,1024,128]{2,1,0:T(8,128)(2,1)} %get-tuple-element.4) | data formatting | bytes 2097152
  64.8 0.0 copy-done
  64.8 0.6 copy.9
Async XLA Ops:
  62.5 2.3 %copy-start = (f32[4,1024]{1,0:T(4,128)S(1)}, f32[4,1024]{1,0:T(4,128)}, u32[]{:S(2)}) copy-start(f32[4,1024]{1,0:T(4,128)} %get-tuple-element.5) | copy-start | bytes 49156

commit v3 on v2

--- a/solution.py
+++ b/solution.py
@@ -79,24 +79,38 @@
 
     pl.semaphore_wait(barrier, sum(cond.astype(jnp.int32) for cond, _ in peers))
 
-    def halo_copy(u):
-        return remote(
-            right_hbm.at[line_of(u)], right_v.at[u, pl.ds(0, n)], halo_ss.at[u], halo_rs.at[u],
-            dev(1, me),
-        )
+    last = lines - 1
+
+    def halo_copy(u, c=None):
+        src, dst, sem = right_hbm.at[line_of(u)], right_v.at[u, pl.ds(0, n)], u
+        if c is not None:
+            src = right_hbm.at[line_of(u), pl.ds(c * blk, blk)]
+            dst, sem = right_v.at[u, pl.ds(c * blk, blk)], lines + c
+        return remote(src, dst, halo_ss.at[sem], halo_rs.at[sem], dev(1, me))
+
+    def halo_copies(u):
+        return [halo_copy(u, c) for c in range(nblk)] if u == last else [halo_copy(u)]
 
     def send_halo(u):
         @pl.when(has_r)
         def _():
-            halo_copy(u).start()
+            for copy in halo_copies(u):
+                copy.start()
 
     send_halo(0)
 
     def mt_up(u):
         return remote(own_mt.at[u], halo_in.at[u], mt_ss.at[u, 0], mt_rs.at[u, 0], dev(1, me))
 
-    def mt_down(u):
-        return remote(halo_mt.at[u], own_in.at[u], mt_ss.at[u, 1], mt_rs.at[u, 1], dev(-1, me))
+    def mt_down(u, c=None):
+        src, dst, sem = halo_mt.at[u], own_in.at[u], u
+        if c is not None:
+            cols = pl.ds(c * blk, blk)
+            src, dst, sem = halo_mt.at[u, :, cols], own_in.at[u, :, cols], lines + c
+        return remote(src, dst, mt_ss.at[sem, 1], mt_rs.at[sem, 1], dev(-1, me))
+
+    def mt_downs(u):
+        return [mt_down(u, c) for c in range(nblk)] if u == last else [mt_down(u)]
 
     def c2_up(u):
         return remote(own_c2.at[u], halo_c2_in.at[u], c2_ss.at[u, 0], c2_rs.at[u, 0], dev(1, me))
@@ -114,17 +128,19 @@
                 routes.append((u, 2 * lines + REACH - 1 - u, None, 2, mate))
         return routes
 
-    def line_copies(u_pick, slots=None):
+    def line_copies(u_pick, slots=None, edges=None):
         copies = []
         for u, slot, cond, to, ln in line_routes():
             if u_pick is not None and u != u_pick or slots is not None and slot not in slots:
                 continue
             mine = u + REACH
             cond = me >= 0 if cond is None else cond
-            if to:
+            if to and edges is not True:
                 copies.append((cond, cond, remote(
                     x0.at[mine, pl.ds(PAD, n)], x0.at[slot, pl.ds(PAD, n)],
                     ln_ss.at[u, to, 0], ln_rs.at[slot, 0], dev(0, ln))))
+            if edges is False:
+                continue
             copies.append((cond & has_r, cond & has_l, remote(
                 x0.at[mine, pl.ds(n, PAD)], x0.at[slot, pl.ds(0, PAD)],
                 ln_ss.at[u, to, 1], ln_rs.at[slot, 1], dev(1, ln))))
@@ -166,10 +182,10 @@
     il = lax.broadcasted_iota(jnp.int32, (blk // 2, blk), 0)
     jl = lax.broadcasted_iota(jnp.int32, (blk // 2, blk), 1)
 
-    def partial_lse(u, own):
+    def partial_lse(u, own, chunks=tuple(range(nblk))):
         base = n if own else 0
         dst = own_mt if own else halo_mt
-        for c in range(nblk):
+        for c in chunks:
             cols = right_v[u, base + c * blk : base + (c + 1) * blk, :]
             pieces = []
             top = jnp.full((8, blk), NEG, F32)
@@ -199,7 +215,7 @@
         tot = a[1:2] * jnp.exp2(a[0:1] - m) + b[1:2] * jnp.exp2(b[0:1] - m)
         return -(m + jnp.log(tot) * LOG2E)
 
-    rows_at = min(64, blk)
+    rows_at = min(128, blk)
     steps = n // rows_at
     tiles = [slice(j * 128, min(win, (j + 1) * 128)) for j in range(-(-win // 128))]
 
@@ -226,7 +242,7 @@
             pot = c1[:, pl.ds(pot_at(k) + tile.start, width)]
             t = groups(s_ref[u, here, tile]) + pot[None]
             e = jnp.exp2(t - top[:, :, :width])
-            k_ref[u % 2, here, tile] = e.reshape(rows_at, width)
+            k_ref[u % 3, here, tile] = e.reshape(rows_at, width)
             if width < 128:
                 e = jnp.concatenate([e, jnp.zeros(e.shape[:2] + (128 - width,), F32)], axis=2)
             total = e if total is None else total + e
@@ -236,17 +252,22 @@
         here = pl.ds(pl.multiple_of(k * rows_at, rows_at), rows_at)
         for tile in tiles:
             width = tile.stop - tile.start
-            part = jnp.sum(groups(k_ref[u % 2, here, tile]) * inv[:, :, :width], axis=0)
+            part = jnp.sum(groups(k_ref[u % 3, here, tile]) * inv[:, :, :width], axis=0)
             c2acc[:, pl.ds(pot_at(k) + tile.start, width)] += part
 
-    def row_pass(u):
-        own = col_pot(own_mt[u], own_in[u])
+    def row_halo(u):
         halo = jnp.where(has_l, col_pot(halo_mt[u], halo_in[u]), NEG)
-        c1[:, n : 2 * n] = jnp.broadcast_to(own, (8, n))
         c1[:, 0:n] = jnp.broadcast_to(halo, (8, n))
         c2acc[...] = jnp.zeros((8, 2 * n), F32)
-        inv = row_exp(u, 0, row_max(u, 0))
-        top = row_max(u, 1)
+
+    def row_own(u, c0, c1_):
+        cols = slice(c0 * blk, c1_ * blk)
+        own = col_pot(own_mt[u, :, cols], own_in[u, :, cols])
+        c1[:, n + c0 * blk : n + c1_ * blk] = jnp.broadcast_to(own, (8, (c1_ - c0) * blk))
+
+    def row_rows(u, first, stop):
+        inv = row_exp(u, first, row_max(u, first))
+        top = row_max(u, first + 1)
 
         def step(k, carry):
             top, inv = carry
@@ -254,9 +275,12 @@
             inv = row_exp(u, k - 1, top)
             return row_max(u, k), inv
 
-        top, inv = lax.fori_loop(2, steps, step, (top, inv))
-        col_sum(u, steps - 2, inv)
-        col_sum(u, steps - 1, row_exp(u, steps - 1, top))
+        if stop > first + 2:
+            top, inv = lax.fori_loop(first + 2, stop, step, (top, inv))
+        col_sum(u, stop - 2, inv)
+        col_sum(u, stop - 1, row_exp(u, stop - 1, top))
+
+    def row_done(u):
         halo_c2[u] = jnp.sum(c2acc[:, 0:n], axis=0, keepdims=True)
         own_c2[u] = jnp.sum(c2acc[:, n : 2 * n], axis=0, keepdims=True)
 
@@ -268,7 +292,7 @@
         ln = line_of(u)
 
         for at in range(0, n, blk):
-            q = groups(k_ref[u % 2, pl.ds(at, blk), :]) * c1[:, pl.ds(at, win)][None]
+            q = groups(k_ref[u % 3, pl.ds(at, blk), :]) * c1[:, pl.ds(at, win)][None]
             q = q.reshape(blk, win).astype(BF16)
             rhs = jnp.concatenate([right_v[u, pl.ds(at, win), :], tcol[pl.ds(at, win), :]], axis=1)
             o = jnp.dot(q, rhs, preferred_element_type=F32)
@@ -306,34 +330,47 @@
                          (3 * h + b) * chans : (3 * h + b + 1) * chans] = w
 
     def scores_step(u):
+        for i, (copy, send) in enumerate(zip(halo_copies(u), mt_downs(u))):
+            @pl.when(has_l)
+            def _():
+                copy.wait_recv()
+
+            partial_lse(u, False, (i,) if u == last else tuple(range(nblk)))
+
+            @pl.when(has_l)
+            def _():
+                send.start()
+
+    def send_c2(u):
+        row_done(u)
+
+        @pl.when(has_r)
+        def _():
+            c2_up(u).start()
+
         @pl.when(has_l)
         def _():
-            halo_copy(u).wait_recv()
-
-        partial_lse(u, False)
-
+            c2_down(u).start()
+
+    def row_first(u):
         @pl.when(has_l)
         def _():
-            mt_down(u).start()
+            mt_up(u).wait_recv()
+
+        row_halo(u)
+
+    def mt_arrived(copies):
+        @pl.when(has_r)
+        def _():
+            for copy in copies:
+                copy.wait_recv()
 
     def row_step(u):
-        @pl.when(has_l)
-        def _():
-            mt_up(u).wait_recv()
-
-        @pl.when(has_r)
-        def _():
-            mt_down(u).wait_recv()
-
-        row_pass(u)
-
-        @pl.when(has_r)
-        def _():
-            c2_up(u).start()
-
-        @pl.when(has_l)
-        def _():
-            c2_down(u).start()
+        row_first(u)
+        mt_arrived(mt_downs(u))
+        row_own(u, 0, nblk)
+        row_rows(u, 0, steps)
+        send_c2(u)
 
     def plan_step(u):
         @pl.when(has_l)
@@ -350,8 +387,8 @@
             def _():
                 copy.start()
 
-    def wait_slots(slots):
-        for _, cond, copy in line_copies(None, slots):
+    def wait_slots(slots, edges):
+        for _, cond, copy in line_copies(None, slots, edges):
             @pl.when(cond)
             def _():
                 copy.wait_recv()
@@ -359,8 +396,12 @@
     part = wide // 3 if (wide // 3) % 16 == 0 else wide
     step_rows = 96
 
-    def conv_pair(src, k, slot, store):
-        for g in range(wide // part):
+    def conv_pair(src, k, slot, store, new_slots=()):
+        count = wide // part
+        for i in range(count):
+            if i == 1 and new_slots:
+                wait_slots(new_slots, True)
+            g = (i + count // 2) % count
             rows = slice(g * part, (g + 1) * part)
             ins = jnp.concatenate([src[slot - 1 + i, rows, :] for i in range(4)], axis=1)
             y = jnp.dot(ins, wbig[k], preferred_element_type=F32)
@@ -394,12 +435,14 @@
             def _():
                 dst[first:stop] = jnp.zeros((stop - first, wide, chans), BF16)
 
-    def layer_pair(src, dst, k, first):
+    def layer_pair(src, dst, k, first, new_slots=()):
+        wait_slots(new_slots, False)
+
         def keep(h, src, slot, bias):
             for at in range(0, wide, step_rows):
                 dst[slot, at : at + step_rows, :] = updated(h, src, slot, bias, at, step_rows)
 
-        conv_pair(src, k, first, keep)
+        conv_pair(src, k, first, keep, new_slots)
         clear_edges(dst, first, first + 2)
 
     def put(h, src, slot, bias):
@@ -413,19 +456,28 @@
             row_step(u - 1)
         if u + 2 < lines:
             send_halo(u + 2)
-        if u >= 2:
+        if u >= 2 and u < last:
             plan_step(u - 2)
-    row_step(lines - 1)
+    per = blk // rows_at
+    row_first(last)
+    mt_arrived(mt_downs(last)[:-1])
+    row_own(last, 0, nblk - 1)
+    row_rows(last, 0, steps - per)
+    mt_arrived(mt_downs(last)[-1:])
+    row_own(last, nblk - 1, nblk)
+    if per == 1:
+        col_sum(last, steps - 1, row_exp(last, steps - 1, row_max(last, steps - 1)))
+    else:
+        row_rows(last, steps - per, steps)
+    send_c2(last)
+    plan_step(lines - 3)
     plan_step(lines - 2)
-    wait_slots((2, 3, 4, 5))
-    layer_pair(x0, x1, 0, 3)
-    plan_step(lines - 1)
-    wait_slots((0, 1))
-    layer_pair(x0, x1, 0, 1)
+    plan_step(last)
+    layer_pair(x0, x1, 0, 3, (2, 3, 4, 5))
+    layer_pair(x0, x1, 0, 1, (0, 1))
     layer_pair(x1, x2, 1, 2)
-    wait_slots((6, 7, 8, 9))
-    layer_pair(x0, x1, 0, 5)
-    layer_pair(x0, x1, 0, 7)
+    layer_pair(x0, x1, 0, 5, (6, 7))
+    layer_pair(x0, x1, 0, 7, (8, 9))
     layer_pair(x1, x2, 1, 4)
     layer_pair(x1, x2, 1, 6)
     conv_pair(x2, 2, 3, put)
@@ -434,14 +486,16 @@
     @pl.when(has_r)
     def _():
         for u in range(lines):
-            halo_copy(u).wait_send()
+            for copy in halo_copies(u):
+                copy.wait_send()
             mt_up(u).wait_send()
             c2_up(u).wait_send()
 
     @pl.when(has_l)
     def _():
         for u in range(lines):
-            mt_down(u).wait_send()
+            for copy in mt_downs(u):
+                copy.wait_send()
             c2_down(u).wait_send()
 
     for cond, _, copy in line_copies(None):
@@ -472,7 +526,7 @@
             vm((lines, 2 * n, chans), BF16),
             vm((2 * n, chans), BF16),
             vm((lines, n, n + blk), F32),
-            vm((2, n, n + blk), F32),
+            vm((3, n, n + blk), F32),
             vm((lines, 2, n), F32),
             vm((lines, 2, n), F32),
             vm((lines, 2, n), F32),
@@ -491,10 +545,10 @@
             vm((6, wide + 16, chans), F32),
             dma((lines, 2)),
             dma,
-            dma((lines,)),
-            dma((lines,)),
-            dma((lines, 2)),
-            dma((lines, 2)),
+            dma((lines + 4,)),
+            dma((lines + 4,)),
+            dma((lines + 4, 2)),
+            dma((lines + 4, 2)),
             dma((lines, 2)),
             dma((lines, 2)),
             dma((lines, 3, 3)),

time: 65.6 us -> 64.6 us (0.985)
  the two profiles are of different devices: /device:TPU:7 before, /device:TPU:29 now
where the time goes in v3:
time: 64.6 us; the launch traced here: 64.4 us
  Pallas kernels  60.9 us (94%)
  local copies, waits for them, and re-layouts  2.88 us (4%)
  between operations  0.65 us (1%)
    pallas_call x1, Pallas kernels, shards(): pl.pallas_call(functools.partial(body, shape), out_shape=(jax.ShapeDtypeS...  60.9 us
    unnamed x4, local copies, waits for them, and re-layouts  2.88 us

profile of v3, /device:TPU:29, one launch (start us, length us, event | category | flops | bytes accessed | tf_op | source)
XLA Modules:
  0.0 64.4 jit_solution(3176295633950407350)
XLA Ops:
  0.6 60.9 %stereo.1 = (bf16[4,1024,128]{2,1,0:T(8,128)(2,1)}, f32[4,1024]{1,0:T(4,128)}) custom-call(bf16[4,1024,128]{2,1,0:T(8,128)(2,1)} %left_hbm.1, bf16[4,1024,128]{2,1,0:T(8,128)(2,1)} %right_hbm.1, bf16[3,3,3,128,128]{4,3,2,1,0:T(8,128)(2,1)} %w_hbm.1, f32[3,128]{1,0:T(4,128)} %bias_ref.1), custom_call_target="tpu_custom_call" | custom-call | tf_op jit(solution)/shard_map/stereo/pallas_call | solution.py:516
  61.6 0.0 copy-start
  61.6 2.3 %copy.8 = bf16[4,1024,128]{2,1,0:T(8,128)(2,1)} copy(bf16[4,1024,128]{2,1,0:T(8,128)(2,1)} %get-tuple-element.4) | data formatting | bytes 2097152
  63.8 0.0 copy-done
  63.8 0.6 copy.9
Async XLA Ops:
  61.6 2.3 %copy-start = (f32[4,1024]{1,0:T(4,128)S(1)}, f32[4,1024]{1,0:T(4,128)}, u32[]{:S(2)}) copy-start(f32[4,1024]{1,0:T(4,128)} %get-tuple-element.5) | copy-start | bytes 49156

commit v4 on v3

--- a/solution.py
+++ b/solution.py
@@ -59,7 +59,7 @@
     barrier = pltpu.get_barrier_semaphore()
     peers = []
     for ds, side in ((-1, has_l), (1, has_r)):
-        peers += [(side, dev(ds, me)), (side, dev(ds, mate)), (side & has_x, dev(ds, cross))]
+        peers += [(side, dev(ds, me))]
     peers += [(me >= 0, dev(0, mate)), (has_x, dev(0, cross))]
     for cond, where in peers:
         @pl.when(cond)
@@ -81,23 +81,29 @@
 
     last = lines - 1
 
-    def halo_copy(u, c=None):
-        src, dst, sem = right_hbm.at[line_of(u)], right_v.at[u, pl.ds(0, n)], u
-        if c is not None:
-            src = right_hbm.at[line_of(u), pl.ds(c * blk, blk)]
-            dst, sem = right_v.at[u, pl.ds(c * blk, blk)], lines + c
-        return remote(src, dst, halo_ss.at[sem], halo_rs.at[sem], dev(1, me))
-
     def halo_copies(u):
-        return [halo_copy(u, c) for c in range(nblk)] if u == last else [halo_copy(u)]
-
-    def send_halo(u):
+        count = nblk if u == last else 2
+        size = n // count
+        return [
+            remote(
+                right_hbm.at[line_of(u), pl.ds(c * size, size)],
+                right_v.at[u, pl.ds(c * size, size)],
+                halo_ss.at[u, c], halo_rs.at[u, c], dev(1, me),
+            )
+            for c in range(count)
+        ]
+
+    def send_halo(u, half):
+        copies = halo_copies(u)
+        per_half = len(copies) // 2
+
         @pl.when(has_r)
         def _():
-            for copy in halo_copies(u):
+            for copy in copies[half * per_half : (half + 1) * per_half]:
                 copy.start()
 
-    send_halo(0)
+    send_halo(0, 0)
+    send_halo(0, 1)
 
     def mt_up(u):
         return remote(own_mt.at[u], halo_in.at[u], mt_ss.at[u, 0], mt_rs.at[u, 0], dev(1, me))
@@ -316,7 +322,7 @@
         return carry
 
     lax.fori_loop(0, lines, own_step, 0)
-    send_halo(1)
+    send_halo(1, 0)
 
     wload.wait()
     wbig[...] = jnp.zeros(wbig.shape, BF16)
@@ -330,10 +336,14 @@
                          (3 * h + b) * chans : (3 * h + b + 1) * chans] = w
 
     def scores_step(u):
-        for i, (copy, send) in enumerate(zip(halo_copies(u), mt_downs(u))):
+        halves = halo_copies(u)
+        sends = mt_downs(u)
+        per_send = len(halves) // len(sends)
+        for i, send in enumerate(sends):
             @pl.when(has_l)
             def _():
-                copy.wait_recv()
+                for copy in halves[i * per_send : (i + 1) * per_send]:
+                    copy.wait_recv()
 
             partial_lse(u, False, (i,) if u == last else tuple(range(nblk)))
 
@@ -450,14 +460,20 @@
         for at in range(0, n, 128):
             out_ref[ln, at : at + 128, :] = updated(h, src, slot, bias, at + PAD, 128)
 
-    for u in range(lines):
-        scores_step(u)
-        if u >= 1:
-            row_step(u - 1)
-        if u + 2 < lines:
-            send_halo(u + 2)
-        if u >= 2 and u < last:
-            plan_step(u - 2)
+    scores_step(0)
+    send_halo(1, 1)
+    send_halo(2, 0)
+    scores_step(1)
+    send_halo(2, 1)
+    row_step(0)
+    send_halo(3, 0)
+    scores_step(2)
+    send_halo(3, 1)
+    row_step(1)
+    plan_step(0)
+    scores_step(3)
+    row_step(2)
+    plan_step(1)
     per = blk // rows_at
     row_first(last)
     mt_arrived(mt_downs(last)[:-1])
@@ -470,9 +486,8 @@
     else:
         row_rows(last, steps - per, steps)
     send_c2(last)
-    plan_step(lines - 3)
-    plan_step(lines - 2)
-    plan_step(last)
+    plan_step(2)
+    plan_step(3)
     layer_pair(x0, x1, 0, 3, (2, 3, 4, 5))
     layer_pair(x0, x1, 0, 1, (0, 1))
     layer_pair(x1, x2, 1, 2)
@@ -545,8 +560,8 @@
             vm((6, wide + 16, chans), F32),
             dma((lines, 2)),
             dma,
-            dma((lines + 4,)),
-            dma((lines + 4,)),
+            dma((lines, 4)),
+            dma((lines, 4)),
             dma((lines + 4, 2)),
             dma((lines + 4, 2)),
             dma((lines, 2)),

time: 64.6 us -> 61.8 us (0.957)
  the two profiles are of different devices: /device:TPU:29 before, /device:TPU:7 now
where the time goes in v4:
time: 61.8 us; the launch traced here: 61.5 us
  Pallas kernels  58 us (94%)
  local copies, waits for them, and re-layouts  2.88 us (5%)
  between operations  0.65 us (1%)
    pallas_call x1, Pallas kernels, shards(): pl.pallas_call(functools.partial(body, shape), out_shape=(jax.ShapeDtypeS...  58 us
    unnamed x4, local copies, waits for them, and re-layouts  2.88 us

profile of v4, /device:TPU:7, one launch (start us, length us, event | category | flops | bytes accessed | tf_op | source)
XLA Modules:
  0.0 61.5 jit_solution(9562367192786957821)
XLA Ops:
  0.6 58.0 %stereo.1 = (bf16[4,1024,128]{2,1,0:T(8,128)(2,1)}, f32[4,1024]{1,0:T(4,128)}) custom-call(bf16[4,1024,128]{2,1,0:T(8,128)(2,1)} %left_hbm.1, bf16[4,1024,128]{2,1,0:T(8,128)(2,1)} %right_hbm.1, bf16[3,3,3,128,128]{4,3,2,1,0:T(8,128)(2,1)} %w_hbm.1, f32[3,128]{1,0:T(4,128)} %bias_ref.1), custom_call_target="tpu_custom_call" | custom-call | tf_op jit(solution)/shard_map/stereo/pallas_call | solution.py:531
  58.6 0.0 copy-start
  58.7 2.3 %copy.8 = bf16[4,1024,128]{2,1,0:T(8,128)(2,1)} copy(bf16[4,1024,128]{2,1,0:T(8,128)(2,1)} %get-tuple-element.4) | data formatting | bytes 2097152
  60.9 0.0 copy-done
  60.9 0.6 copy.9
Async XLA Ops:
  58.6 2.3 %copy-start = (f32[4,1024]{1,0:T(4,128)S(1)}, f32[4,1024]{1,0:T(4,128)}, u32[]{:S(2)}) copy-start(f32[4,1024]{1,0:T(4,128)} %get-tuple-element.5) | copy-start | bytes 49156

commit v5 on v4

--- a/solution.py
+++ b/solution.py
@@ -26,10 +26,11 @@
 
 
 def body(
-    shape, left_hbm, right_hbm, w_hbm, bias_ref, out_ref, disp_ref,
+    shape, left_hbm, right_hbm, w_hbm, bias_ref, out_hbm, disp_hbm,
     left_v, right_v, tcol, s_ref, k_ref, own_mt, halo_mt, own_in, halo_in, c1, c2acc,
     own_c2, halo_c2, own_c2_in, halo_c2_in, w_v, wbig, x0, x1, x2, y_ref,
     load_sem, wsem, halo_ss, halo_rs, mt_ss, mt_rs, c2_ss, c2_rs, ln_ss, ln_rs,
+    out_ref, disp_ref, out_sem,
 ):
     segs, line_devs, lines, n, blk, chans, layers = shape
     nblk = n // blk
@@ -455,10 +456,13 @@
         conv_pair(src, k, first, keep, new_slots)
         clear_edges(dst, first, first + 2)
 
+    def line_out(u):
+        return pltpu.make_async_copy(out_ref.at[u], out_hbm.at[line_of(u)], out_sem.at[u])
+
     def put(h, src, slot, bias):
-        ln = line_of(slot - REACH)
         for at in range(0, n, 128):
-            out_ref[ln, at : at + 128, :] = updated(h, src, slot, bias, at + PAD, 128)
+            out_ref[slot - REACH, at : at + 128, :] = updated(h, src, slot, bias, at + PAD, 128)
+        line_out(slot - REACH).start()
 
     scores_step(0)
     send_halo(1, 1)
@@ -473,7 +477,6 @@
     plan_step(0)
     scores_step(3)
     row_step(2)
-    plan_step(1)
     per = blk // rows_at
     row_first(last)
     mt_arrived(mt_downs(last)[:-1])
@@ -486,8 +489,11 @@
     else:
         row_rows(last, steps - per, steps)
     send_c2(last)
+    plan_step(1)
     plan_step(2)
     plan_step(3)
+    disp_out = pltpu.make_async_copy(disp_ref, disp_hbm, out_sem.at[lines])
+    disp_out.start()
     layer_pair(x0, x1, 0, 3, (2, 3, 4, 5))
     layer_pair(x0, x1, 0, 1, (0, 1))
     layer_pair(x1, x2, 1, 2)
@@ -497,6 +503,9 @@
     layer_pair(x1, x2, 1, 6)
     conv_pair(x2, 2, 3, put)
     conv_pair(x2, 2, 5, put)
+    disp_out.wait()
+    for u in range(lines):
+        line_out(u).wait()
 
     @pl.when(has_r)
     def _():
@@ -517,6 +526,27 @@
         @pl.when(cond)
         def _():
             copy.wait_send()
+
+
+def hand_over(pieces, src, disp_src, dst, disp_dst, hold, disp_hold, in_sem, out_sem):
+    lines, n, _ = src.shape
+    size = lines * n // pieces
+    spots = [(k * size // n, pl.ds(k * size % n, size)) for k in range(pieces)]
+    loads = [
+        pltpu.make_async_copy(src.at[at], hold.at[at], in_sem.at[k]) for k, at in enumerate(spots)
+    ]
+    stores = [
+        pltpu.make_async_copy(hold.at[at], dst.at[at], out_sem.at[k]) for k, at in enumerate(spots)
+    ]
+    loads.append(pltpu.make_async_copy(disp_src, disp_hold, in_sem.at[pieces]))
+    stores.append(pltpu.make_async_copy(disp_hold, disp_dst, out_sem.at[pieces]))
+    for load in loads:
+        load.start()
+    for load, store in zip(loads, stores):
+        load.wait()
+        store.start()
+    for store in stores:
+        store.wait()
 
 
 def shards(segs, line_devs, left, right, weight, bias):
@@ -528,14 +558,14 @@
     shape = (segs, line_devs, lines, n, blk, chans, layers)
     dma = pltpu.SemaphoreType.DMA
     vm = pltpu.VMEM
-    return pl.pallas_call(
+    refined, disparity = pl.pallas_call(
         functools.partial(body, shape),
         out_shape=(
             jax.ShapeDtypeStruct((lines, n, chans), BF16),
             jax.ShapeDtypeStruct((lines, n), F32),
         ),
         in_specs=[pl.BlockSpec(memory_space=pl.ANY)] * 3 + [pl.BlockSpec(memory_space=vm)],
-        out_specs=(pl.BlockSpec(memory_space=vm), pl.BlockSpec(memory_space=vm)),
+        out_specs=(pl.BlockSpec(memory_space=pl.ANY), pl.BlockSpec(memory_space=pl.ANY)),
         scratch_shapes=[
             vm((lines, n, chans), BF16),
             vm((lines, 2 * n, chans), BF16),
@@ -568,12 +598,32 @@
             dma((lines, 2)),
             dma((lines, 3, 3)),
             dma((slots, 3)),
+            vm((lines, n, chans), BF16),
+            vm((lines, n), F32),
+            dma((lines + 1,)),
         ],
         compiler_params=pltpu.CompilerParams(
             collective_id=0, has_side_effects=True, vmem_limit_bytes=60 * 1024 * 1024
         ),
         name="stereo",
     )(left, right, weight, bias)
+    pieces = 8
+    return pl.pallas_call(
+        functools.partial(hand_over, pieces),
+        out_shape=(
+            jax.ShapeDtypeStruct((lines, n, chans), BF16),
+            jax.ShapeDtypeStruct((lines, n), F32),
+        ),
+        in_specs=[pl.BlockSpec(memory_space=pl.ANY)] * 2,
+        out_specs=(pl.BlockSpec(memory_space=pl.ANY), pl.BlockSpec(memory_space=pl.ANY)),
+        scratch_shapes=[
+            vm((lines, n, chans), BF16),
+            vm((lines, n), F32),
+            dma((pieces + 1,)),
+            dma((pieces + 1,)),
+        ],
+        name="hand_over",
+    )(refined, disparity)
 
 
 def solution(mesh):

time: 61.8 us -> 64.1 us (1.037)
  the two profiles are of different devices: /device:TPU:7 before, /device:TPU:61 now
where the time goes in v5:
time: 64.1 us; the launch traced here: 64 us
  Pallas kernels  63.2 us (99%)
  between operations  0.8 us (1%)
    pallas_call x1, Pallas kernels, shards(): pl.pallas_call(functools.partial(body, shape), out_shape=(jax.ShapeDtypeS...  61.1 us
    pallas_call x1, Pallas kernels, shards(): pl.pallas_call(functools.partial(hand_over, pieces), out_shape=(jax.Shape...  2.11 us

profile of v5, /device:TPU:61, one launch (start us, length us, event | category | flops | bytes accessed | tf_op | source)
XLA Modules:
  0.0 64.0 jit_solution(16392937273985847904)
XLA Ops:
  0.6 61.1 %stereo.1 = (bf16[4,1024,128]{2,1,0:T(8,128)(2,1)}, f32[4,1024]{1,0:T(4,128)}) custom-call(bf16[4,1024,128]{2,1,0:T(8,128)(2,1)} %left_hbm.1, bf16[4,1024,128]{2,1,0:T(8,128)(2,1)} %right_hbm.1, bf16[3,3,3,128,128]{4,3,2,1,0:T(8,128)(2,1)} %w_hbm.1, f32[3,128]{1,0:T(4,128)} %bias_ref.1), custom_call_target="tpu_custom_call" | custom-call | tf_op jit(solution)/shard_map/stereo/pallas_call | solution.py:561
  61.7 2.1 %hand_over.1 = (bf16[4,1024,128]{2,1,0:T(8,128)(2,1)}, f32[4,1024]{1,0:T(4,128)}) custom-call(bf16[4,1024,128]{2,1,0:T(8,128)(2,1)} %get-tuple-element.4.src, f32[4,1024]{1,0:T(4,128)} %get-tuple-element.5.disp_src), custom_call_target="tpu_custom_call" | custom-call | tf_op jit(solution)/shard_map/hand_over/pallas_call | solution.py:611

commit v6 on v5

--- a/solution.py
+++ b/solution.py
@@ -477,6 +477,7 @@
     plan_step(0)
     scores_step(3)
     row_step(2)
+    plan_step(1)
     per = blk // rows_at
     row_first(last)
     mt_arrived(mt_downs(last)[:-1])
@@ -489,7 +490,6 @@
     else:
         row_rows(last, steps - per, steps)
     send_c2(last)
-    plan_step(1)
     plan_step(2)
     plan_step(3)
     disp_out = pltpu.make_async_copy(disp_ref, disp_hbm, out_sem.at[lines])

time: 64.1 us -> 61.3 us (0.956)
  the two profiles are of different devices: /device:TPU:61 before, /device:TPU:7 now
where the time goes in v6:
time: 61.3 us; the launch traced here: 61 us
  Pallas kernels  60.2 us (98%)
  between operations  0.8 us (1%)
    pallas_call x1, Pallas kernels, shards(): pl.pallas_call(functools.partial(body, shape), out_shape=(jax.ShapeDtypeS...  58.1 us
    pallas_call x1, Pallas kernels, shards(): pl.pallas_call(functools.partial(hand_over, pieces), out_shape=(jax.Shape...  2.11 us

profile of v6, /device:TPU:7, one launch (start us, length us, event | category | flops | bytes accessed | tf_op | source)
XLA Modules:
  0.0 61.0 jit_solution(6041130026625747141)
XLA Ops:
  0.6 58.1 %stereo.1 = (bf16[4,1024,128]{2,1,0:T(8,128)(2,1)}, f32[4,1024]{1,0:T(4,128)}) custom-call(bf16[4,1024,128]{2,1,0:T(8,128)(2,1)} %left_hbm.1, bf16[4,1024,128]{2,1,0:T(8,128)(2,1)} %right_hbm.1, bf16[3,3,3,128,128]{4,3,2,1,0:T(8,128)(2,1)} %w_hbm.1, f32[3,128]{1,0:T(4,128)} %bias_ref.1), custom_call_target="tpu_custom_call" | custom-call | tf_op jit(solution)/shard_map/stereo/pallas_call | solution.py:561
  58.7 2.1 %hand_over.1 = (bf16[4,1024,128]{2,1,0:T(8,128)(2,1)}, f32[4,1024]{1,0:T(4,128)}) custom-call(bf16[4,1024,128]{2,1,0:T(8,128)(2,1)} %get-tuple-element.4.src, f32[4,1024]{1,0:T(4,128)} %get-tuple-element.5.disp_src), custom_call_target="tpu_custom_call" | custom-call | tf_op jit(solution)/shard_map/hand_over/pallas_call | solution.py:611

commit v7 on v6

--- a/solution.py
+++ b/solution.py
@@ -105,6 +105,7 @@
 
     send_halo(0, 0)
     send_halo(0, 1)
+    send_halo(1, 0)
 
     def mt_up(u):
         return remote(own_mt.at[u], halo_in.at[u], mt_ss.at[u, 0], mt_rs.at[u, 0], dev(1, me))
@@ -323,7 +324,6 @@
         return carry
 
     lax.fori_loop(0, lines, own_step, 0)
-    send_halo(1, 0)
 
     wload.wait()
     wbig[...] = jnp.zeros(wbig.shape, BF16)

time: 61.3 us -> 61.3 us (level)
  no operation moved by 1% of the time
where the time goes in v7:
time: 61.3 us; the launch traced here: 61 us
  Pallas kernels  60.2 us (98%)
  between operations  0.8 us (1%)
    pallas_call x1, Pallas kernels, shards(): pl.pallas_call(functools.partial(body, shape), out_shape=(jax.ShapeDtypeS...  58.1 us
    pallas_call x1, Pallas kernels, shards(): pl.pallas_call(functools.partial(hand_over, pieces), out_shape=(jax.Shape...  2.11 us

profile of v7, /device:TPU:7, one launch (start us, length us, event | category | flops | bytes accessed | tf_op | source)
XLA Modules:
  0.0 61.0 jit_solution(5835220656834681833)
XLA Ops:
  0.6 58.1 %stereo.1 = (bf16[4,1024,128]{2,1,0:T(8,128)(2,1)}, f32[4,1024]{1,0:T(4,128)}) custom-call(bf16[4,1024,128]{2,1,0:T(8,128)(2,1)} %left_hbm.1, bf16[4,1024,128]{2,1,0:T(8,128)(2,1)} %right_hbm.1, bf16[3,3,3,128,128]{4,3,2,1,0:T(8,128)(2,1)} %w_hbm.1, f32[3,128]{1,0:T(4,128)} %bias_ref.1), custom_call_target="tpu_custom_call" | custom-call | tf_op jit(solution)/shard_map/stereo/pallas_call | solution.py:561
  58.7 2.1 %hand_over.1 = (bf16[4,1024,128]{2,1,0:T(8,128)(2,1)}, f32[4,1024]{1,0:T(4,128)}) custom-call(bf16[4,1024,128]{2,1,0:T(8,128)(2,1)} %get-tuple-element.4.src, f32[4,1024]{1,0:T(4,128)} %get-tuple-element.5.disp_src), custom_call_target="tpu_custom_call" | custom-call | tf_op jit(solution)/shard_map/hand_over/pallas_call | solution.py:611
